TPU v7x, 256 devices: a whole 4x4x8 slice. The times are simulated.
256 devices in a mesh: slab: 32 (over y, x, z_lo), blk: 8 (over z_hi, core).
Axes of the slice: x: 4, y: 4, z: 8 (z_hi: 4, z_lo: 2; z = z_hi * 2 + z_lo), core: 2. Of those that a mesh axis runs over, the one named last changes fastest.
Arguments:
- interior: float32 [64, 512, 512], P('slab', 'blk'), may hold values from -6 to 6
- sources: float32 [64, 512, 512], P('slab', 'blk'), may hold values from -12 to 12
- absorption: float32 [64, 512, 512], P('slab', 'blk'), may hold values from 0.1 to 4
- bem_panel: bfloat16 [8192, 131072], P('blk', 'slab'), may hold values from -0.03125 to 0.03125
- incident: bfloat16 [131072, 512], P('slab'), may hold values from -160 to 160
- node_cell: int32 [131072], P('slab'), may hold values from 0 to 255
- offset: int32 [1], replicated, may hold values from 0 to 122880, as said below
Outputs:
- relaxed: float32 [64, 512, 512], P('slab', 'blk')
- boundary_flux: float32 [8192, 512], P(('blk', 'slab'))
Inputs may be any that keep to these rules, and one draw needn't show every extreme that they name: offset is a multiple of 8192; rows offset to offset + 8191 lie among the 131072 boundary nodes.
All inputs are finite; a program needn't handle non-finite values.
Results may differ from a plain program's by a relative error of at most 0.0034.
Values sent between devices are 32-bit elements; how exact they have to be, the bound alone decides.
A program may use at most 64 MiB of HBM per device.

v0:
```python
import jax
import jax.numpy as jnp
from jax import lax
from jax.sharding import PartitionSpec as P

SWEEPS = 2
omega = 0.6
center_weight = 8.0 / 3.0


def padded_2(cells, sides, width):
    for axis, dim in sides:
        count = lax.axis_size(axis)
        ends = count - 1
        head = lax.slice_in_dim(cells, 0, width, axis=dim)
        tail = lax.slice_in_dim(cells, cells.shape[dim] - width, cells.shape[dim], axis=dim)
        cells = jnp.concatenate(
            [
                lax.ppermute(tail, axis, [(i, (i + 1) % count) for i in range(ends)]),
                cells,
                lax.ppermute(head, axis, [((i + 1) % count, i) for i in range(ends)]),
            ],
            axis=dim,
        )
    return cells


def stiffness(padded):
    along_x = padded[:, :, :-2] + padded[:, :, 2:]
    middle = padded[:, :, 1:-1]
    plus_mid = along_x + middle
    plane_sum = plus_mid[:, :-2] + plus_mid[:, 1:-1] + plus_mid[:, 2:]
    total_sum = plane_sum[:-2] + plane_sum[1:-1] + plane_sum[2:]
    cross_xy = along_x[:, :-2] + along_x[:, 2:]
    corner_sum = cross_xy[:-2] + cross_xy[2:]
    face_sum = (
        along_x[1:-1, 1:-1]
        + middle[1:-1, :-2]
        + middle[1:-1, 2:]
        + middle[:-2, 1:-1]
        + middle[2:, 1:-1]
    )
    center = middle[1:-1, 1:-1]
    edge_sum = total_sum - center - face_sum - corner_sum
    return center_weight * center - edge_sum / 6.0 - corner_sum / 12.0


def sweep_once(padded, sources, absorption):
    center = padded[1:-1, 1:-1, 1:-1]
    applied = stiffness(padded) + absorption * center
    return center + omega * (sources - applied) / (center_weight + absorption)


def pad_x(values):
    return jnp.pad(values, ((0, 0), (0, 0), (1, 1)))


def per_device(interior, sources, absorption, bem_panel, incident, node_cell, offset):
    depth_z, depth_y, width_x = interior.shape
    current = interior
    for sweep_idx in range(SWEEPS):
        padded = padded_2(current, (("slab", 0), ("blk", 1)), 1)
        current = sweep_once(pad_x(padded), sources, absorption)
    slab_cols = incident.shape[0]
    own_count = slab_cols // lax.axis_size("blk")
    x_faces = jnp.stack([interior[:, :, 0], interior[:, :, width_x - 1]], axis=-1).reshape(-1)
    own_cells = lax.dynamic_slice_in_dim(node_cell, lax.axis_index("blk") * own_count, own_count, 0)
    own_trace = jnp.take(x_faces, own_cells, axis=0)
    trace = lax.all_gather(own_trace, "blk", axis=0, tiled=True)
    fields = (incident.astype(jnp.float32) + trace[:, None]).astype(jnp.bfloat16)
    wide = fields.astype(jnp.float32)
    node_total = slab_cols * lax.axis_size("slab")
    squares = lax.psum(jnp.sum(wide * wide, axis=0), "slab")
    norms = jnp.sqrt(squares / node_total + 1e-06)
    panel_rows = bem_panel.shape[0]
    first_col = lax.axis_index("slab") * slab_cols
    shift_rows = offset[0] + lax.axis_index("blk") * panel_rows - first_col
    share = panel_rows // lax.axis_size("slab")
    product = jnp.dot(bem_panel, fields, preferred_element_type=jnp.float32)
    node_pos = shift_rows + jnp.arange(panel_rows, dtype=jnp.int32)
    valid = (node_pos >= 0) & (node_pos < slab_cols)
    picked = jnp.take(wide, jnp.clip(node_pos, 0, slab_cols - 1), axis=0)
    summed = product + 0.5 * jnp.where(valid[:, None], picked, 0.0)
    summed = summed / norms[None, :]
    summed_all = lax.psum(summed, "slab")
    owned = lax.dynamic_slice_in_dim(summed_all, lax.axis_index("slab") * share, share, 0)
    return (current, owned)


def solution(mesh):
    in_specs = (
        P("slab", "blk", None),
        P("slab", "blk", None),
        P("slab", "blk", None),
        P("blk", "slab"),
        P("slab", None),
        P("slab"),
        P(),
    )
    out_specs = (P("slab", "blk", None), P(("blk", "slab"), None))
    return jax.shard_map(
        per_device, mesh=mesh, in_specs=in_specs, out_specs=out_specs, check_vma=False
    )
```

profile of v0, /device:TPU:32, one launch (start us, length us, event | category | flops | bytes accessed | tf_op | source)
XLA Modules:
  0.0 480.4 jit_solution(14701295206737365730)
XLA Ops:
  7.2 1.0 fusion.47
  8.2 2.9 collective-permute-start
  11.2 2.9 collective-permute-start.1
  14.1 1.0 fusion.45
  16.0 0.1 reshape.43
  16.1 0.8 compare_select_fusion.2
  16.9 3.5 gather_fusion
  20.4 0.8 and_select_fusion
  21.2 17.4 %all-gather = f32[8,1,512]{2,1,0:T(1,128)S(1)} all-gather(f32[1,1,512]{2,1,0:T(1,128)S(1)} %bitcast.13), channel_id=1, replica_groups=mesh['slab'=32,'blk'=8] {'blk'}, dimensions={0}, use_global_device_ids=true | all-gather | bytes 18432 | tf_op jit(solution)/shard_map/all_gather | solution.py:69
  38.6 5.4 %multiply_reduce_fusion = (f32[512]{0:T(512)S(1)}, f32[4096,512]{1,0:T(8,128)}) fusion(f32[4096]{0:T(1024)S(1)} %bitcast.10, bf16[4096,512]{1,0:T(8,128)(2,1)} %param.11), kind=kLoop, calls=%fused_computation.2 | loop fusion | flops 12582400 | bytes 12601344 | tf_op jit(solution)/shard_map/reduce_sum | solution.py:73
  44.0 79.4 %psum.14 = f32[512]{0:T(512)S(1)} all-reduce(f32[512]{0:T(512)S(1)} %get-tuple-element.12), channel_id=1, replica_groups=mesh['slab'=32,'blk'=8] {'slab'}, use_global_device_ids=true, to_apply=%region_1.2 | all-reduce | flops 512 | bytes 4096 | tf_op jit(solution)/shard_map/psum | solution.py:73
  123.4 7.4 %gather_fusion.1 = f32[1024,512]{1,0:T(8,128)S(1)} fusion(f32[4096,512]{1,0:T(8,128)} %get-tuple-element.13, s32[1024]{0:T(1024)S(1)} %get-tuple-element.27), kind=kCustom, calls=%fused_computation.1 | custom fusion | bytes 4198400 | tf_op jit(solution)/shard_map/jit(_take)/gather | solution.py:82
  130.9 1.9 copy.16
  132.9 1.3 collective-permute-start.2
  134.2 1.3 collective-permute-start.3
  135.5 11.9 %fusion = f32[1024,512]{0,1:T(8,128)} fusion(f32[1024,512]{0,1:T(8,128)} %copy.16, bf16[1024,4096]{1,0:T(8,128)(2,1)} %param.10, f32[512]{0:T(512)S(1)} %add_sqrt_fusion, pred[1024]{0:T(1024)(128)(4,1)S(1)} %get-tuple-element.28, pred[1024]{0:T(1024)(128)(4,1)S(1)} %get-tuple-element.29, bf16[4096,512]{1,0:T(8,128)(2,1)} %param.11, f32[4096]{0:T(1024)S(1)} %bitcast.11), kind=kOutput, calls=%fused_computation.5 | convolution fusion | flops 4303880192 | bytes 16797696 | tf_op jit(solution)/shard_map/dot_general | solution.py:79
  147.5 0.4 fusion.39
  147.9 0.2 slice_add_fusion.3
  148.1 0.2 copy-done.1
  148.4 0.3 fusion.28
  148.8 2.9 collective-permute-start.4
  151.7 4.7 collective-permute-start.5
  156.4 1.5 collective-permute-done.4
  157.9 2.7 collective-permute-done.5
  160.6 2.1 collective-permute-start.6
  162.7 1.3 collective-permute-start.7
  164.0 4.8 collective-permute-done.7
  168.8 0.4 fusion.40
  169.4 1.0 fusion.13
  170.4 301.3 %all-reduce.4.cloned.1.call-done = f32[1024,512]{0,1:T(8,128)} async-done(((f32[1024,512]{0,1:T(8,128)}), f32[1024,512]{0,1:T(8,128)}) %all-reduce.4.cloned.1.call-update) | async-done | bytes 2097168 | tf_op jit(solution)/shard_map/psum | solution.py:85
  471.7 1.1 constant_dynamic-slice_fusion
  472.8 0.7 copy.17
  (30 shorter events, 0.9 us)
Async XLA Ops:
  7.2 464.6 %all-reduce.4.cloned.1.call-start = ((), (), s32[]{:S(2)}) async-start(), calls=%async_computation | async-start | bytes 4194304 | tf_op jit(solution)/shard_map/psum | solution.py:85
  8.2 124.5 %collective-permute-start = (f32[1,64,512]{2,1,0:T(8,128)S(1)}, f32[1,64,512]{2,1,0:T(8,128)S(1)}, u32[]{:S(2)}, u32[]{:S(2)}) collective-permute-start(f32[1,64,512]{2,1,0:T(8,128)S(1)} %get-tuple-element.22), channel_id=1, source_target_pairs={{0,8},{8,16},{16,24},{24,32},{32,40},{40,48},{48,56},{56,64},{64,7... | collective-permute-start | bytes 393224 | tf_op jit(solution)/shard_map/ppermute | solution.py:19
  11.2 121.7 %collective-permute-start.1 = (f32[1,64,512]{2,1,0:T(8,128)S(1)}, f32[1,64,512]{2,1,0:T(8,128)S(1)}, u32[]{:S(2)}, u32[]{:S(2)}) collective-permute-start(f32[1,64,512]{2,1,0:T(8,128)S(1)} %get-tuple-element.23), channel_id=1, source_target_pairs={{8,0},{16,8},{24,16},{32,24},{40,32},{48,40},{56,48},{64,56},{72,6... | collective-permute-start | bytes 393224 | tf_op jit(solution)/shard_map/ppermute | solution.py:21
  130.9 1.9 copy-start
  132.9 14.6 %collective-permute-start.2 = (f32[4,1,512]{2,1,0:T(1,128)S(1)}, f32[4,1,512]{2,1,0:T(1,128)S(1)}, u32[]{:S(2)}, u32[]{:S(2)}) collective-permute-start(f32[4,1,512]{2,1,0:T(1,128)S(1)} %get-tuple-element.16), channel_id=1, source_target_pairs={{0,1},{1,2},{2,3},{3,4},{4,5},{5,6},{6,7},{8,9},{9,10},{10,11},{11... | collective-permute-start | bytes 24584 | tf_op jit(solution)/shard_map/ppermute | solution.py:19
  134.2 13.3 %collective-permute-start.3 = (f32[4,1,512]{2,1,0:T(1,128)S(1)}, f32[4,1,512]{2,1,0:T(1,128)S(1)}, u32[]{:S(2)}, u32[]{:S(2)}) collective-permute-start(f32[4,1,512]{2,1,0:T(1,128)S(1)} %get-tuple-element.17), channel_id=1, source_target_pairs={{1,0},{2,1},{3,2},{4,3},{5,4},{6,5},{7,6},{9,8},{10,9},{11,10},{12... | collective-permute-start | bytes 24584 | tf_op jit(solution)/shard_map/ppermute | solution.py:21
  147.4 0.9 copy-start.1
  147.4 1.0 copy-start.2
  148.8 9.1 %collective-permute-start.4 = (f32[1,64,512]{2,1,0:T(8,128)S(1)}, f32[1,64,512]{2,1,0:T(8,128)S(1)}, u32[]{:S(2)}, u32[]{:S(2)}) collective-permute-start(f32[1,64,512]{2,1,0:T(8,128)S(1)} %get-tuple-element.20), channel_id=1, source_target_pairs={{0,8},{8,16},{16,24},{24,32},{32,40},{40,48},{48,56},{56,64},{64,7... | collective-permute-start | bytes 393224 | tf_op jit(solution)/shard_map/ppermute | solution.py:19
  151.7 8.8 %collective-permute-start.5 = (f32[1,64,512]{2,1,0:T(8,128)S(1)}, f32[1,64,512]{2,1,0:T(8,128)S(1)}, u32[]{:S(2)}, u32[]{:S(2)}) collective-permute-start(f32[1,64,512]{2,1,0:T(8,128)S(1)} %get-tuple-element.21), channel_id=1, source_target_pairs={{8,0},{16,8},{24,16},{32,24},{40,32},{48,40},{56,48},{64,56},{72,6... | collective-permute-start | bytes 393224 | tf_op jit(solution)/shard_map/ppermute | solution.py:21
  160.6 3.4 collective-permute-start.6
  162.7 6.1 %collective-permute-start.7 = (f32[4,1,512]{2,1,0:T(1,128)S(1)}, f32[4,1,512]{2,1,0:T(1,128)S(1)}, u32[]{:S(2)}, u32[]{:S(2)}) collective-permute-start(f32[4,1,512]{2,1,0:T(1,128)S(1)} %get-tuple-element.15), channel_id=1, source_target_pairs={{1,0},{2,1},{3,2},{4,3},{5,4},{6,5},{7,6},{9,8},{10,9},{11,10},{12... | collective-permute-start | bytes 24584 | tf_op jit(solution)/shard_map/ppermute | solution.py:21
Sparse Core Ops, SparseCore 0:
  147.6 324.1 all-reduce.3
where the time goes:
time: 481 us; the launch traced here: 480 us
  waiting for transfers between devices  310 us (64%)
  blocking collectives  96.8 us (20%)
  starting transfers between devices  19.4 us (4%)
  local copies, waits for them, and re-layouts  17.3 us (4%)
  between operations  15 us (3%)
  matrix products  11.9 us (2%)
  other arithmetic  9.66 us (2%)
    psum x1, waiting for transfers between devices, per_device(): summed_all = lax.psum(summed, 'slab')  301 us
    psum x1, blocking collectives, per_device(): squares = lax.psum(jnp.sum(wide * wide, axis=0), 'slab')  79.4 us
    all_gather x1, blocking collectives, per_device(): trace = lax.all_gather(own_trace, 'blk', axis=0, tiled=True)  17.4 us
    dot_general x1, matrix products, per_device(): product = jnp.dot(bem_panel, fields, preferred_element_type=jnp.float32)  11.9 us
    ppermute x4, starting transfers between devices, padded_2(): lax.ppermute(head, axis, [((i + 1) % count, i) for i in range(ends)])  10.1 us
  transfers between devices with their start and end apart: 9, of which 4 were waited for; matrix products, arithmetic and copies ran while one was open for 7% of the time, Pallas kernels for 0%

commit v1 on v0

--- a/solution.py
+++ b/solution.py
@@ -66,7 +66,9 @@
     x_faces = jnp.stack([interior[:, :, 0], interior[:, :, width_x - 1]], axis=-1).reshape(-1)
     own_cells = lax.dynamic_slice_in_dim(node_cell, lax.axis_index("blk") * own_count, own_count, 0)
     own_trace = jnp.take(x_faces, own_cells, axis=0)
-    trace = lax.all_gather(own_trace, "blk", axis=0, tiled=True)
+    trace = jnp.concatenate(
+        lax.all_to_all(jnp.stack([own_trace] * lax.axis_size("blk")), "blk", 0, 0), axis=0
+    )
     fields = (incident.astype(jnp.float32) + trace[:, None]).astype(jnp.bfloat16)
     wide = fields.astype(jnp.float32)
     node_total = slab_cols * lax.axis_size("slab")

time: 481 us -> 475 us (0.988)
  blocking collectives: 96.8 us -> 78.5 us
  starting transfers between devices: 19.4 us -> 29.6 us
    all_gather x1 -> x0, blocking collectives: 17.4 us -> none  [per_device(): trace = lax.all_gather(own_trace, 'blk', axis=0, tiled=True)]
    all_to_all x0 -> x1, starting transfers between devices: none -> 7.57 us  [per_device(): lax.all_to_all(jnp.stack([own_trace] * lax.axis_size('blk')), 'blk', 0, 0)]
  transfers between devices with their start and end apart: 9 -> 10, of which waited for: 4 -> 5; matrix products, arithmetic and copies ran while one was open for 7% -> 6% of each run, Pallas kernels for 0% -> 0%
where the time goes in v1:
time: 475 us
  waiting for transfers between devices  312 us (66%)
  blocking collectives  78.5 us (17%)
  starting transfers between devices  29.6 us (6%)
  local copies, waits for them, and re-layouts  17.9 us (4%)
  between operations  15 us (3%)
  matrix products  11.9 us (3%)
  other arithmetic  9.67 us (2%)
    psum x1, waiting for transfers between devices, per_device(): summed_all = lax.psum(summed, 'slab')  302 us
    psum x1, blocking collectives, per_device(): squares = lax.psum(jnp.sum(wide * wide, axis=0), 'slab')  78.5 us
    ppermute x4, starting transfers between devices, padded_2(): lax.ppermute(tail, axis, [(i, (i + 1) % count) for i in range(ends)])  12.8 us
    dot_general x1, matrix products, per_device(): product = jnp.dot(bem_panel, fields, preferred_element_type=jnp.float32)  11.9 us
  transfers between devices with their start and end apart: 10, of which 5 were waited for; matrix products, arithmetic and copies ran while one was open for 6% of the time, Pallas kernels for 0%

profile of v1, /device:TPU:32, one launch (start us, length us, event | category | flops | bytes accessed | tf_op | source)
XLA Modules:
  0.0 474.8 jit_solution(15005128021981897233)
XLA Ops:
  7.8 1.0 fusion.45
  9.2 0.8 compare_select_fusion.2
  10.0 3.5 gather_fusion
  13.5 0.8 and_select_fusion
  14.3 0.6 stack.5
  14.9 7.6 %all-to-all-start = ((f32[8,1,512]{2,1,0:T(1,128)}), f32[8,1,512]{2,1,0:T(1,128)S(1)}, u32[]{:S(2)}, u32[]{:S(2)}) async-start(f32[8,1,512]{2,1,0:T(1,128)} %stack.5), calls=%async_computation | async-start | bytes 32768 | tf_op jit(solution)/shard_map/all_to_all | solution.py:70
  22.5 1.0 fusion.47
  23.5 3.8 collective-permute-start
  27.4 2.0 collective-permute-start.1
  29.4 0.9 all-to-all-done
  30.3 5.4 %multiply_reduce_fusion = (f32[512]{0:T(512)S(1)}, f32[4096,512]{1,0:T(8,128)}) fusion(f32[4096]{0:T(1024)S(1)} %bitcast.9, bf16[4096,512]{1,0:T(8,128)(2,1)} %param.11), kind=kLoop, calls=%fused_computation.2 | loop fusion | flops 12582400 | bytes 12601344 | tf_op jit(solution)/shard_map/reduce_sum | solution.py:75
  35.7 7.4 %gather_fusion.1 = f32[1024,512]{1,0:T(8,128)S(1)} fusion(f32[4096,512]{1,0:T(8,128)} %get-tuple-element.13, s32[1024]{0:T(1024)S(1)} %get-tuple-element.27), kind=kCustom, calls=%fused_computation.1 | custom fusion | bytes 4198400 | tf_op jit(solution)/shard_map/jit(_take)/gather | solution.py:84
  43.1 1.8 copy.16
  45.0 78.5 %psum.14 = f32[512]{0:T(512)S(1)} all-reduce(f32[512]{0:T(512)S(1)} %get-tuple-element.12), channel_id=1, replica_groups=mesh['slab'=32,'blk'=8] {'slab'}, use_global_device_ids=true, to_apply=%region_1.2 | all-reduce | flops 512 | bytes 4096 | tf_op jit(solution)/shard_map/psum | solution.py:75
  123.7 1.3 collective-permute-start.2
  125.0 1.3 collective-permute-start.3
  126.3 11.9 %fusion = f32[1024,512]{0,1:T(8,128)} fusion(f32[1024,512]{0,1:T(8,128)} %copy.16, bf16[1024,4096]{1,0:T(8,128)(2,1)} %param.10, f32[512]{0:T(512)S(1)} %add_sqrt_fusion, pred[1024]{0:T(1024)(128)(4,1)S(1)} %get-tuple-element.28, pred[1024]{0:T(1024)(128)(4,1)S(1)} %get-tuple-element.29, bf16[4096,512]{1,0:T(8,128)(2,1)} %param.11, f32[4096]{0:T(1024)S(1)} %bitcast.10), kind=kOutput, calls=%fused_computation.5 | convolution fusion | flops 4303880192 | bytes 16797696 | tf_op jit(solution)/shard_map/dot_general | solution.py:81
  138.3 0.4 fusion.39
  138.9 0.2 copy-done.1
  139.2 0.3 fusion.28
  139.6 3.8 collective-permute-start.4
  143.4 4.7 collective-permute-start.5
  148.1 1.0 collective-permute-done.4
  149.1 2.1 collective-permute-done.5
  151.2 3.8 collective-permute-start.6
  155.0 1.3 collective-permute-start.7
  156.3 6.5 %collective-permute-done.7 = f32[4,1,512]{2,1,0:T(1,128)S(1)} collective-permute-done((f32[4,1,512]{2,1,0:T(1,128)S(1)}, f32[4,1,512]{2,1,0:T(1,128)S(1)}, u32[]{:S(2)}, u32[]{:S(2)}) %collective-permute-start.7) | collective-permute-done | bytes 8224 | tf_op jit(solution)/shard_map/ppermute | solution.py:21
  162.9 0.4 fusion.40
  163.5 1.0 fusion.13
  164.5 301.6 %all-reduce.4.cloned.1.call-done = f32[1024,512]{0,1:T(8,128)} async-done(((f32[1024,512]{0,1:T(8,128)}), f32[1024,512]{0,1:T(8,128)}) %all-reduce.4.cloned.1.call-update) | async-done | bytes 2097168 | tf_op jit(solution)/shard_map/psum | solution.py:87
  466.2 1.1 constant_dynamic-slice_fusion
  467.3 0.7 copy.17
  (32 shorter events, 1.2 us)
Async XLA Ops:
  14.9 15.4 %all-to-all-start = ((f32[8,1,512]{2,1,0:T(1,128)}), f32[8,1,512]{2,1,0:T(1,128)S(1)}, u32[]{:S(2)}, u32[]{:S(2)}) async-start(f32[8,1,512]{2,1,0:T(1,128)} %stack.5), calls=%async_computation | async-start | bytes 32768 | tf_op jit(solution)/shard_map/all_to_all | solution.py:70
  22.5 443.7 %all-reduce.4.cloned.1.call-start = ((), (), s32[]{:S(2)}) async-start(), calls=%async_computation.1 | async-start | bytes 4194304 | tf_op jit(solution)/shard_map/psum | solution.py:87
  23.5 100.0 %collective-permute-start = (f32[1,64,512]{2,1,0:T(8,128)S(1)}, f32[1,64,512]{2,1,0:T(8,128)S(1)}, u32[]{:S(2)}, u32[]{:S(2)}) collective-permute-start(f32[1,64,512]{2,1,0:T(8,128)S(1)} %get-tuple-element.22), channel_id=1, source_target_pairs={{0,8},{8,16},{16,24},{24,32},{32,40},{40,48},{48,56},{56,64},{64,7... | collective-permute-start | bytes 393224 | tf_op jit(solution)/shard_map/ppermute | solution.py:19
  27.4 96.2 %collective-permute-start.1 = (f32[1,64,512]{2,1,0:T(8,128)S(1)}, f32[1,64,512]{2,1,0:T(8,128)S(1)}, u32[]{:S(2)}, u32[]{:S(2)}) collective-permute-start(f32[1,64,512]{2,1,0:T(8,128)S(1)} %get-tuple-element.23), channel_id=1, source_target_pairs={{8,0},{16,8},{24,16},{32,24},{40,32},{48,40},{56,48},{64,56},{72,6... | collective-permute-start | bytes 393224 | tf_op jit(solution)/shard_map/ppermute | solution.py:21
  43.1 80.4 %copy-start = (f32[2,64,512]{2,1,0:T(8,128)S(1)}, f32[2,64,512]{2,1,0:T(8,128)}, u32[]{:S(2)}) copy-start(f32[2,64,512]{2,1,0:T(8,128)} %param.7) | copy-start | bytes 786436
  123.7 14.6 %collective-permute-start.2 = (f32[4,1,512]{2,1,0:T(1,128)S(1)}, f32[4,1,512]{2,1,0:T(1,128)S(1)}, u32[]{:S(2)}, u32[]{:S(2)}) collective-permute-start(f32[4,1,512]{2,1,0:T(1,128)S(1)} %get-tuple-element.16), channel_id=1, source_target_pairs={{0,1},{1,2},{2,3},{3,4},{4,5},{5,6},{6,7},{8,9},{9,10},{10,11},{11... | collective-permute-start | bytes 24584 | tf_op jit(solution)/shard_map/ppermute | solution.py:19
  125.0 13.3 %collective-permute-start.3 = (f32[4,1,512]{2,1,0:T(1,128)S(1)}, f32[4,1,512]{2,1,0:T(1,128)S(1)}, u32[]{:S(2)}, u32[]{:S(2)}) collective-permute-start(f32[4,1,512]{2,1,0:T(1,128)S(1)} %get-tuple-element.17), channel_id=1, source_target_pairs={{1,0},{2,1},{3,2},{4,3},{5,4},{6,5},{7,6},{9,8},{10,9},{11,10},{12... | collective-permute-start | bytes 24584 | tf_op jit(solution)/shard_map/ppermute | solution.py:21
  138.2 0.9 copy-start.1
  138.2 1.0 copy-start.2
  139.6 9.5 %collective-permute-start.4 = (f32[1,64,512]{2,1,0:T(8,128)S(1)}, f32[1,64,512]{2,1,0:T(8,128)S(1)}, u32[]{:S(2)}, u32[]{:S(2)}) collective-permute-start(f32[1,64,512]{2,1,0:T(8,128)S(1)} %get-tuple-element.20), channel_id=1, source_target_pairs={{0,8},{8,16},{16,24},{24,32},{32,40},{40,48},{48,56},{56,64},{64,7... | collective-permute-start | bytes 393224 | tf_op jit(solution)/shard_map/ppermute | solution.py:19
  143.4 7.8 %collective-permute-start.5 = (f32[1,64,512]{2,1,0:T(8,128)S(1)}, f32[1,64,512]{2,1,0:T(8,128)S(1)}, u32[]{:S(2)}, u32[]{:S(2)}) collective-permute-start(f32[1,64,512]{2,1,0:T(8,128)S(1)} %get-tuple-element.21), channel_id=1, source_target_pairs={{8,0},{16,8},{24,16},{32,24},{40,32},{48,40},{56,48},{64,56},{72,6... | collective-permute-start | bytes 393224 | tf_op jit(solution)/shard_map/ppermute | solution.py:21
  151.2 5.2 %collective-permute-start.6 = (f32[4,1,512]{2,1,0:T(1,128)S(1)}, f32[4,1,512]{2,1,0:T(1,128)S(1)}, u32[]{:S(2)}, u32[]{:S(2)}) collective-permute-start(f32[4,1,512]{2,1,0:T(1,128)S(1)} %get-tuple-element.14), channel_id=1, source_target_pairs={{0,1},{1,2},{2,3},{3,4},{4,5},{5,6},{6,7},{8,9},{9,10},{10,11},{11... | collective-permute-start | bytes 24584 | tf_op jit(solution)/shard_map/ppermute | solution.py:19
  155.0 7.8 %collective-permute-start.7 = (f32[4,1,512]{2,1,0:T(1,128)S(1)}, f32[4,1,512]{2,1,0:T(1,128)S(1)}, u32[]{:S(2)}, u32[]{:S(2)}) collective-permute-start(f32[4,1,512]{2,1,0:T(1,128)S(1)} %get-tuple-element.15), channel_id=1, source_target_pairs={{1,0},{2,1},{3,2},{4,3},{5,4},{6,5},{7,6},{9,8},{10,9},{11,10},{12... | collective-permute-start | bytes 24584 | tf_op jit(solution)/shard_map/ppermute | solution.py:21
Sparse Core Ops, SparseCore 0:
  138.3 327.7 all-reduce.3
